TPU v7x, 256 devices: a whole 4x4x8 slice. The times are simulated.
256 devices in a mesh: rows: 32 (over z, x), feat: 8 (over y, core).
Axes of the slice: x: 4, y: 4, z: 8, core: 2. Of those that a mesh axis runs over, the one named last changes fastest.
Arguments:
- points: float32 [8, 131072], P(None, 'rows'), may hold values from -4 to 4
- freq_index: int32 [8, 16384], P(None, 'feat'), may hold values from -12 to 12
- log_density: float32 [16384], P('feat'), may hold values from -3 to 2.7
- targets: float32 [131072], P('rows'), may hold values from -16 to 16
- probes: int32 [31, 131072], P(None, 'rows'), may hold values 0 or 1
Outputs:
- solution: float32 [32, 131072], P(None, 'rows')
- residual: float32 [32, 131072], P(None, 'rows')
All inputs are finite; a program needn't handle non-finite values. No bound on the sum of `probes` on one device may be relied on, other than what follows from the above.
Results may differ from a plain program's by a relative error of at most 0.0025.
Values may be sent and summed in bfloat16 or wider, within the bound.
A program may use at most 128 MiB of HBM per device.

v0:
```python
import math
import jax
import jax.numpy as jnp
from jax import lax
from jax.sharding import PartitionSpec as P

FREQS = 16384
ITERS = 2
frequency_step = 0.25
noise_level = 1.0


def build_features(points, frequency, amplitude, block_rows):
    rows_here = points.shape[1]
    blocks = rows_here // block_rows
    feature_width = 2 * frequency.shape[1]

    def fill(block_index, table):
        first_row = (block_index * block_rows).astype(jnp.int32)
        point_block = lax.dynamic_slice_in_dim(points, first_row, block_rows, 1)
        phases = jnp.dot(
            point_block.T,
            frequency,
            precision=lax.Precision.HIGHEST,
            preferred_element_type=jnp.float32,
        )
        block = jnp.concatenate(
            [amplitude * jnp.cos(phases), amplitude * jnp.sin(phases)], axis=1
        ).astype(jnp.bfloat16)
        return lax.dynamic_update_slice_in_dim(table, block, first_row, 0)

    initial = jnp.zeros((rows_here, feature_width), jnp.bfloat16)
    return lax.fori_loop(0, blocks, fill, initial)


def squared_norm(values):
    return lax.psum(jnp.sum(values * values, axis=1), "rows")


def local(points, freq_index, log_density, targets, probes):
    rows_here = points.shape[1]
    block_rows = math.gcd(rows_here, 512)
    frequency = frequency_step * freq_index.astype(jnp.float32)
    amplitude = jnp.exp(0.5 * log_density) / math.sqrt(FREQS)
    features = build_features(points, frequency, amplitude, block_rows)
    right_sides = jnp.concatenate([targets[None, :], (2 * probes - 1).astype(jnp.float32)], axis=0)
    solution = jnp.zeros_like(right_sides)
    residual = right_sides
    direction = right_sides
    residual_energy = squared_norm(right_sides)
    for iteration in range(ITERS):
        direction_bf = direction.astype(jnp.bfloat16)
        partial_coeffs = jnp.dot(direction_bf, features, preferred_element_type=jnp.float32)
        coeff_bf = lax.psum(partial_coeffs, "rows").astype(jnp.bfloat16)
        coeff_bf = lax.optimization_barrier(coeff_bf)
        partial_images = lax.dot_general(
            coeff_bf, features, (((1,), (1,)), ((), ())), preferred_element_type=jnp.float32
        )
        coeff_wide = coeff_bf.astype(jnp.float32)
        energy_part = jnp.sum(coeff_wide * coeff_wide, axis=1)
        images = lax.psum(partial_images, "feat")
        feature_energy = lax.psum(energy_part, "feat")
        direction_energy = lax.psum(jnp.sum(direction * direction, axis=1), "rows")
        curvature = feature_energy + noise_level * direction_energy
        step_size = residual_energy / curvature
        solution = solution + step_size[:, None] * direction
        residual = residual - step_size[:, None] * (images + noise_level * direction)
        if iteration + 1 < ITERS:
            energy_next = squared_norm(residual)
            mixing = energy_next / residual_energy
            direction = residual + mixing[:, None] * direction
            residual_energy = energy_next
    return (solution, residual)


def solution(mesh):
    in_specs = (P(None, "rows"), P(None, "feat"), P("feat"), P("rows"), P(None, "rows"))
    out_specs = (P(None, "rows"), P(None, "rows"))
    return jax.shard_map(local, mesh=mesh, in_specs=in_specs, out_specs=out_specs, check_vma=False)
```

profile of v0, /device:TPU:2, one launch (start us, length us, event | category | flops | bytes accessed | tf_op | source)
XLA Modules:
  0.0 764.3 jit_solution(17343094420450126333)
XLA Ops:
  8.8 11.0 %broadcast_in_dim.9 = bf16[4096,4096]{1,0:T(8,128)(2,1)} broadcast(bf16[]{:T(256)} %constant.42.clone.1), dimensions={} | broadcast | bytes 33554432 | tf_op jit(solution)/shard_map/broadcast_in_dim | solution.py:32
  19.7 182.7 %while.13 = (s32[]{:T(128)}, bf16[4096,4096]{1,0:T(8,128)(2,1)}, f32[2048]{0:T(1024)S(1)}, f32[8,4096]{1,0:T(8,128)}, f32[8,2048]{1,0:T(8,128)S(1)}, /*index=5*/s32[]{:T(128)}, s32[]{:T(128)}, s32[]{:T(128)}, s32[]{:T(128)}) while((s32[]{:T(128)}, bf16[4096,4096]{1,0:T(8,128)(2,1)}, f32[2048]{0:T(1024)S(1)}, f32[8,4096]{1,0:T(8,128)}, ...), condition=%wide.region_3.0_spmd, body=%wide.region_2.0_spmd.sunk | while | flops 113246216 | bytes 12673179 | solution.py:33
  19.7 20.4 %multiply_convert_fusion.3 = (bf16[512,2048]{1,0:T(8,128)(2,1)S(1)}, bf16[512,2048]{1,0:T(8,128)(2,1)S(1)}) fusion(f32[2048]{0:T(1024)S(1)} %get-tuple-element.170, f32[8,2048]{1,0:T(8,128)S(1)} %get-tuple-element.172, f32[8,4096]{1,0:T(8,128)} %get-tuple-element.171, s32[]{:T(128)S(6)} %select_n.9), kind=kOutput, calls=%fused_computation.2.clone.1 | convolution fusion | flops 104857600 | bytes 4284420 | tf_op jit(solution)/shard_map/while/body/eval_jaxpr/dot_general | solution.py:21
  42.6 20.4 %multiply_convert_fusion.3 = (bf16[512,2048]{1,0:T(8,128)(2,1)S(1)}, bf16[512,2048]{1,0:T(8,128)(2,1)S(1)}) fusion(f32[2048]{0:T(1024)S(1)} %get-tuple-element.170, f32[8,2048]{1,0:T(8,128)S(1)} %get-tuple-element.172, f32[8,4096]{1,0:T(8,128)} %get-tuple-element.171, s32[]{:T(128)S(6)} %select_n.9), kind=kOutput, calls=%fused_computation.2.clone.1 | convolution fusion | flops 104857600 | bytes 4284420 | tf_op jit(solution)/shard_map/while/body/eval_jaxpr/dot_general | solution.py:21
  63.0 2.5 maximum_dynamic-update-slice_fusion.2
  65.4 20.4 %multiply_convert_fusion.3 = (bf16[512,2048]{1,0:T(8,128)(2,1)S(1)}, bf16[512,2048]{1,0:T(8,128)(2,1)S(1)}) fusion(f32[2048]{0:T(1024)S(1)} %get-tuple-element.170, f32[8,2048]{1,0:T(8,128)S(1)} %get-tuple-element.172, f32[8,4096]{1,0:T(8,128)} %get-tuple-element.171, s32[]{:T(128)S(6)} %select_n.9), kind=kOutput, calls=%fused_computation.2.clone.1 | convolution fusion | flops 104857600 | bytes 4284420 | tf_op jit(solution)/shard_map/while/body/eval_jaxpr/dot_general | solution.py:21
  85.8 2.5 maximum_dynamic-update-slice_fusion.2
  88.3 20.4 %multiply_convert_fusion.3 = (bf16[512,2048]{1,0:T(8,128)(2,1)S(1)}, bf16[512,2048]{1,0:T(8,128)(2,1)S(1)}) fusion(f32[2048]{0:T(1024)S(1)} %get-tuple-element.170, f32[8,2048]{1,0:T(8,128)S(1)} %get-tuple-element.172, f32[8,4096]{1,0:T(8,128)} %get-tuple-element.171, s32[]{:T(128)S(6)} %select_n.9), kind=kOutput, calls=%fused_computation.2.clone.1 | convolution fusion | flops 104857600 | bytes 4284420 | tf_op jit(solution)/shard_map/while/body/eval_jaxpr/dot_general | solution.py:21
  111.1 20.4 %multiply_convert_fusion.3 = (bf16[512,2048]{1,0:T(8,128)(2,1)S(1)}, bf16[512,2048]{1,0:T(8,128)(2,1)S(1)}) fusion(f32[2048]{0:T(1024)S(1)} %get-tuple-element.170, f32[8,2048]{1,0:T(8,128)S(1)} %get-tuple-element.172, f32[8,4096]{1,0:T(8,128)} %get-tuple-element.171, s32[]{:T(128)S(6)} %select_n.9), kind=kOutput, calls=%fused_computation.2.clone.1 | convolution fusion | flops 104857600 | bytes 4284420 | tf_op jit(solution)/shard_map/while/body/eval_jaxpr/dot_general | solution.py:21
  133.9 20.4 %multiply_convert_fusion.3 = (bf16[512,2048]{1,0:T(8,128)(2,1)S(1)}, bf16[512,2048]{1,0:T(8,128)(2,1)S(1)}) fusion(f32[2048]{0:T(1024)S(1)} %get-tuple-element.170, f32[8,2048]{1,0:T(8,128)S(1)} %get-tuple-element.172, f32[8,4096]{1,0:T(8,128)} %get-tuple-element.171, s32[]{:T(128)S(6)} %select_n.9), kind=kOutput, calls=%fused_computation.2.clone.1 | convolution fusion | flops 104857600 | bytes 4284420 | tf_op jit(solution)/shard_map/while/body/eval_jaxpr/dot_general | solution.py:21
  156.8 20.4 %multiply_convert_fusion.3 = (bf16[512,2048]{1,0:T(8,128)(2,1)S(1)}, bf16[512,2048]{1,0:T(8,128)(2,1)S(1)}) fusion(f32[2048]{0:T(1024)S(1)} %get-tuple-element.170, f32[8,2048]{1,0:T(8,128)S(1)} %get-tuple-element.172, f32[8,4096]{1,0:T(8,128)} %get-tuple-element.171, s32[]{:T(128)S(6)} %select_n.9), kind=kOutput, calls=%fused_computation.2.clone.1 | convolution fusion | flops 104857600 | bytes 4284420 | tf_op jit(solution)/shard_map/while/body/eval_jaxpr/dot_general | solution.py:21
  177.2 2.5 maximum_dynamic-update-slice_fusion.2
  179.6 20.4 %multiply_convert_fusion.3 = (bf16[512,2048]{1,0:T(8,128)(2,1)S(1)}, bf16[512,2048]{1,0:T(8,128)(2,1)S(1)}) fusion(f32[2048]{0:T(1024)S(1)} %get-tuple-element.170, f32[8,2048]{1,0:T(8,128)S(1)} %get-tuple-element.172, f32[8,4096]{1,0:T(8,128)} %get-tuple-element.171, s32[]{:T(128)S(6)} %select_n.9), kind=kOutput, calls=%fused_computation.2.clone.1 | convolution fusion | flops 104857600 | bytes 4284420 | tf_op jit(solution)/shard_map/while/body/eval_jaxpr/dot_general | solution.py:21
  202.7 13.5 %fusion.5 = f32[32,4096]{1,0:T(8,128)S(1)} fusion(bf16[4096,4096]{1,0:T(8,128)(2,1)} %get-tuple-element.96, f32[31,4096]{1,0:T(8,128)S(1)} %add_convert_fusion, f32[1,4096]{1,0:T(1,128)S(1)} %bitcast.11), kind=kOutput, calls=%fused_computation.19 | convolution fusion | flops 1074266112 | bytes 34603008 | tf_op jit(solution)/shard_map/dot_general | solution.py:53
  216.3 146.9 %all-reduce.10 = (bf16[32,4096]{1,0:T(8,128)(2,1)S(1)}, f32[32]{0:T(128)S(1)}) all-reduce(f32[32,4096]{1,0:T(8,128)S(1)} %fusion.5, f32[32]{0:T(128)S(1)} %multiply_reduce_fusion.4), channel_id=1, replica_groups=mesh['rows'=32,'feat'=8] {'rows'}, use_global_device_ids=true, to_apply=%region_4.0 | all-reduce | flops 131104 | bytes 786688 | tf_op jit(solution)/shard_map/psum | solution.py:54
  363.2 16.0 %fusion.8 = f32[32,4096]{1,0:T(8,128)} fusion(bf16[32,4096]{1,0:T(8,128)(2,1)S(1)} %get-tuple-element.109, bf16[4096,4096]{1,0:T(8,128)(2,1)} %get-tuple-element.96), kind=kOutput, calls=%fused_computation.26 | convolution fusion | flops 1073741824 | bytes 34340864 | tf_op jit(solution)/shard_map/dot_general | solution.py:56
  379.5 12.4 %psum.68 = f32[32]{0:T(128)S(1)} all-reduce(f32[32]{0:T(128)S(1)} %multiply_reduce_fusion.3), channel_id=1, replica_groups=mesh['rows'=32,'feat'=8] {'feat'}, use_global_device_ids=true, to_apply=%region_6.0 | all-reduce | flops 32 | bytes 256 | tf_op jit(solution)/shard_map/psum | solution.py:62
  391.9 53.1 %all-reduce.7.cloned.1.call-done = f32[32,4096]{1,0:T(8,128)} async-done(((f32[32,4096]{1,0:T(8,128)}), f32[32,4096]{1,0:T(8,128)}) %all-reduce.7.cloned.1.call-update) | async-done | bytes 524304 | tf_op jit(solution)/shard_map/psum | solution.py:61
  446.4 71.1 %psum.70 = f32[32]{0:T(128)S(1)} all-reduce(f32[32]{0:T(128)S(1)} %multiply_reduce_fusion.2), channel_id=1, replica_groups=mesh['rows'=32,'feat'=8] {'rows'}, use_global_device_ids=true, to_apply=%region_9.0 | all-reduce | flops 32 | bytes 256 | tf_op jit(solution)/shard_map/psum | solution.py:37
  517.5 13.8 %fusion.3 = f32[32,4096]{1,0:T(8,128)S(1)} fusion(bf16[4096,4096]{1,0:T(8,128)(2,1)} %get-tuple-element.96, f32[32]{0:T(128)S(1)} %div.18, f32[31,4096]{1,0:T(8,128)S(1)} %add_convert_fusion, f32[1,4096]{1,0:T(1,128)S(1)} %bitcast.13, f32[32,4096]{1,0:T(8,128)} %all-reduce.7.cloned.1.call-done, f32[32]{0:T(128)S(1)} %add_divide_fusion), kind=kOutput, calls=%fused_computation.17 | convolution fusion | flops 1074659328 | bytes 35127552 | tf_op jit(solution)/shard_map/dot_general | solution.py:53
  531.6 145.0 %all-reduce.11 = (bf16[32,4096]{1,0:T(8,128)(2,1)S(1)}, f32[32]{0:T(128)S(1)}) all-reduce(f32[32,4096]{1,0:T(8,128)S(1)} %fusion.3, f32[32]{0:T(128)S(1)} %multiply_reduce_fusion), channel_id=1, replica_groups=mesh['rows'=32,'feat'=8] {'rows'}, use_global_device_ids=true, to_apply=%region_10.0 | all-reduce | flops 131104 | bytes 786688 | tf_op jit(solution)/shard_map/psum | solution.py:54
  676.6 16.0 %fusion.9 = f32[32,4096]{1,0:T(8,128)} fusion(bf16[32,4096]{1,0:T(8,128)(2,1)S(1)} %get-tuple-element.107, bf16[4096,4096]{1,0:T(8,128)(2,1)} %get-tuple-element.96), kind=kOutput, calls=%fused_computation.27 | convolution fusion | flops 1073741824 | bytes 34340864 | tf_op jit(solution)/shard_map/dot_general | solution.py:56
  692.8 12.4 %psum.72 = f32[32]{0:T(128)S(1)} all-reduce(f32[32]{0:T(128)S(1)} %multiply_reduce_fusion.1), channel_id=1, replica_groups=mesh['rows'=32,'feat'=8] {'feat'}, use_global_device_ids=true, to_apply=%region_12.0 | all-reduce | flops 32 | bytes 256 | tf_op jit(solution)/shard_map/psum | solution.py:62
  705.2 49.9 %all-reduce.9.cloned.1.call-done = f32[32,4096]{1,0:T(8,128)} async-done(((f32[32,4096]{1,0:T(8,128)}), f32[32,4096]{1,0:T(8,128)}) %all-reduce.9.cloned.1.call-update) | async-done | bytes 524304 | tf_op jit(solution)/shard_map/psum | solution.py:61
  (27 shorter events, 18.5 us)
Async XLA Ops:
  7.2 437.9 %all-reduce.7.cloned.1.call-start = ((), (), s32[]{:S(2)}) async-start(), calls=%async_computation | async-start | bytes 1048576 | tf_op jit(solution)/shard_map/psum | solution.py:61
  19.7 182.7 %copy-start.2 = (s32[31,4096]{1,0:T(8,128)S(1)}, s32[31,4096]{1,0:T(8,128)}, u32[]{:S(2)}) copy-start(s32[31,4096]{1,0:T(8,128)} %param.11) | copy-start | bytes 1523716
  19.7 182.8 %copy-start.1 = (f32[4096]{0:T(1024)S(1)}, f32[4096]{0:T(1024)}, u32[]{:S(2)}) copy-start(f32[4096]{0:T(1024)} %param.10) | copy-start | bytes 49156
  379.2 375.9 %all-reduce.9.cloned.1.call-start = ((), (), s32[]{:S(2)}) async-start(), calls=%async_computation.1 | async-start | bytes 1048576 | tf_op jit(solution)/shard_map/psum | solution.py:61
  445.0 86.3 %copy-start = (f32[32,4096]{1,0:T(8,128)S(1)}, f32[32,4096]{1,0:T(8,128)}, u32[]{:S(2)}) copy-start(f32[32,4096]{1,0:T(8,128)} %all-reduce.7.cloned.1.call-done) | copy-start | bytes 1572868
Sparse Core Ops, SparseCore 0:
  379.4 65.6 all-reduce.6
  692.7 62.3 all-reduce.8
where the time goes:
time: 765 us; the launch traced here: 764 us
  blocking collectives  388 us (51%)
  matrix products  222 us (29%)
  waiting for transfers between devices  103 us (13%)
  other arithmetic  25.8 us (3%)
  between operations  14.1 us (2%)
  local copies, waits for them, and re-layouts  11 us (1%)
    psum x2, blocking collectives, local(): coeff_bf = lax.psum(partial_coeffs, 'rows').astype(jnp.bfloat16)  292 us
    dot_general x8, matrix products, fill(): jnp.dot(point_block.T, frequency, precision=lax.Precision.HIGHEST, prefer...  163 us
    psum x2, waiting for transfers between devices, local(): images = lax.psum(partial_images, 'feat')  103 us
    psum x1, blocking collectives, squared_norm(): return lax.psum(jnp.sum(values * values, axis=1), 'rows')  71.1 us
    dot_general x2, matrix products, local(): lax.dot_general(coeff_bf, features, (((1,), (1,)), ((), ())), preferred_e...  32 us
    dot_general x2, matrix products, local(): jnp.dot(direction_bf, features, preferred_element_type=jnp.float32)  27.3 us
    psum x2, blocking collectives, local(): feature_energy = lax.psum(energy_part, 'feat')  24.8 us
    dynamic_update_slice x8, other arithmetic, fill(): return lax.dynamic_update_slice_in_dim(table, block, first_row, 0)  19.7 us
  transfers between devices with their start and end apart: 2, of which 2 were waited for; matrix products, arithmetic and copies ran while one was open for 0% of the time, Pallas kernels for 0%

commit v1 on v0

--- a/solution.py
+++ b/solution.py
@@ -58,7 +58,10 @@
         )
         coeff_wide = coeff_bf.astype(jnp.float32)
         energy_part = jnp.sum(coeff_wide * coeff_wide, axis=1)
-        images = lax.psum(partial_images, "feat")
+        size, images = (lax.axis_size("feat"), partial_images)
+        for far in [1 << k for k in range(size.bit_length() - 1)]:
+            swap = [(i, i ^ far) for i in range(size)]
+            images = images + lax.ppermute(images, "feat", swap)
         feature_energy = lax.psum(energy_part, "feat")
         direction_energy = lax.psum(jnp.sum(direction * direction, axis=1), "rows")
         curvature = feature_energy + noise_level * direction_energy

time: 765 us -> 698 us (0.912)
  waiting for transfers between devices: 103 us -> 28.9 us
  between operations: 14.1 us -> 0.71 us
  blocking collectives: 388 us -> 399 us
  starting transfers between devices: 0.08 us -> 7.93 us
    psum x2 -> x0, waiting for transfers between devices: 103 us -> none  [local(): images = lax.psum(partial_images, 'feat')]
    ppermute x0 -> x6, waiting for transfers between devices: none -> 28.9 us  [local(): images = images + lax.ppermute(images, 'feat', swap)]
    psum x2, blocking collectives: 24.8 us -> 36.6 us  [local(): feature_energy = lax.psum(energy_part, 'feat')]
    ppermute x0 -> x6, starting transfers between devices: none -> 7.93 us  [local(): images = images + lax.ppermute(images, 'feat', swap)]
  transfers between devices with their start and end apart: 2 -> 6, of which waited for: 2 -> 4; matrix products, arithmetic and copies ran while one was open for 0% -> 0% of each run, Pallas kernels for 0% -> 0%
where the time goes in v1:
time: 698 us; the launch traced here: 693 us
  blocking collectives  399 us (57%)
  matrix products  221 us (32%)
  waiting for transfers between devices  28.9 us (4%)
  other arithmetic  24 us (3%)
  local copies, waits for them, and re-layouts  11 us (2%)
  starting transfers between devices  7.93 us (1%)
    psum x2, blocking collectives, local(): coeff_bf = lax.psum(partial_coeffs, 'rows').astype(jnp.bfloat16)  287 us
    dot_general x8, matrix products, fill(): jnp.dot(point_block.T, frequency, precision=lax.Precision.HIGHEST, prefer...  163 us
    psum x1, blocking collectives, squared_norm(): return lax.psum(jnp.sum(values * values, axis=1), 'rows')  75.4 us
    psum x2, blocking collectives, local(): feature_energy = lax.psum(energy_part, 'feat')  36.6 us
    dot_general x2, matrix products, local(): lax.dot_general(coeff_bf, features, (((1,), (1,)), ((), ())), preferred_e...  30.6 us
    ppermute x6, waiting for transfers between devices, local(): images = images + lax.ppermute(images, 'feat', swap)  28.9 us
    dot_general x2, matrix products, local(): jnp.dot(direction_bf, features, preferred_element_type=jnp.float32)  27.1 us
    dynamic_update_slice x8, other arithmetic, fill(): return lax.dynamic_update_slice_in_dim(table, block, first_row, 0)  19.7 us
  transfers between devices with their start and end apart: 6, of which 4 were waited for; matrix products, arithmetic and copies ran while one was open for 0% of the time, Pallas kernels for 0%

profile of v1, /device:TPU:2, one launch (start us, length us, event | category | flops | bytes accessed | tf_op | source)
XLA Modules:
  0.0 692.7 jit_solution(5797195477211097075)
XLA Ops:
  2.2 11.0 %broadcast_in_dim.9 = bf16[4096,4096]{1,0:T(8,128)(2,1)} broadcast(bf16[]{:T(256)} %constant.42.clone.1), dimensions={} | broadcast | bytes 33554432 | tf_op jit(solution)/shard_map/broadcast_in_dim | solution.py:32
  13.2 182.7 %while.13 = (s32[]{:T(128)}, bf16[4096,4096]{1,0:T(8,128)(2,1)}, f32[2048]{0:T(1024)S(1)}, f32[8,4096]{1,0:T(8,128)}, f32[8,2048]{1,0:T(8,128)S(1)}, /*index=5*/s32[]{:T(128)}, s32[]{:T(128)}, s32[]{:T(128)}, s32[]{:T(128)}) while((s32[]{:T(128)}, bf16[4096,4096]{1,0:T(8,128)(2,1)}, f32[2048]{0:T(1024)S(1)}, f32[8,4096]{1,0:T(8,128)}, ...), condition=%wide.region_3.0_spmd, body=%wide.region_2.0_spmd.sunk | while | flops 113246216 | bytes 12673179 | solution.py:33
  13.2 20.4 %multiply_convert_fusion.3 = (bf16[512,2048]{1,0:T(8,128)(2,1)S(1)}, bf16[512,2048]{1,0:T(8,128)(2,1)S(1)}) fusion(f32[2048]{0:T(1024)S(1)} %get-tuple-element.172, f32[8,2048]{1,0:T(8,128)S(1)} %get-tuple-element.174, f32[8,4096]{1,0:T(8,128)} %get-tuple-element.173, s32[]{:T(128)S(6)} %select_n.9), kind=kOutput, calls=%fused_computation.2.clone.1 | convolution fusion | flops 104857600 | bytes 4284420 | tf_op jit(solution)/shard_map/while/body/eval_jaxpr/dot_general | solution.py:21
  36.0 20.4 %multiply_convert_fusion.3 = (bf16[512,2048]{1,0:T(8,128)(2,1)S(1)}, bf16[512,2048]{1,0:T(8,128)(2,1)S(1)}) fusion(f32[2048]{0:T(1024)S(1)} %get-tuple-element.172, f32[8,2048]{1,0:T(8,128)S(1)} %get-tuple-element.174, f32[8,4096]{1,0:T(8,128)} %get-tuple-element.173, s32[]{:T(128)S(6)} %select_n.9), kind=kOutput, calls=%fused_computation.2.clone.1 | convolution fusion | flops 104857600 | bytes 4284420 | tf_op jit(solution)/shard_map/while/body/eval_jaxpr/dot_general | solution.py:21
  58.9 20.4 %multiply_convert_fusion.3 = (bf16[512,2048]{1,0:T(8,128)(2,1)S(1)}, bf16[512,2048]{1,0:T(8,128)(2,1)S(1)}) fusion(f32[2048]{0:T(1024)S(1)} %get-tuple-element.172, f32[8,2048]{1,0:T(8,128)S(1)} %get-tuple-element.174, f32[8,4096]{1,0:T(8,128)} %get-tuple-element.173, s32[]{:T(128)S(6)} %select_n.9), kind=kOutput, calls=%fused_computation.2.clone.1 | convolution fusion | flops 104857600 | bytes 4284420 | tf_op jit(solution)/shard_map/while/body/eval_jaxpr/dot_general | solution.py:21
  79.2 2.5 maximum_dynamic-update-slice_fusion.2
  81.7 20.4 %multiply_convert_fusion.3 = (bf16[512,2048]{1,0:T(8,128)(2,1)S(1)}, bf16[512,2048]{1,0:T(8,128)(2,1)S(1)}) fusion(f32[2048]{0:T(1024)S(1)} %get-tuple-element.172, f32[8,2048]{1,0:T(8,128)S(1)} %get-tuple-element.174, f32[8,4096]{1,0:T(8,128)} %get-tuple-element.173, s32[]{:T(128)S(6)} %select_n.9), kind=kOutput, calls=%fused_computation.2.clone.1 | convolution fusion | flops 104857600 | bytes 4284420 | tf_op jit(solution)/shard_map/while/body/eval_jaxpr/dot_general | solution.py:21
  104.6 20.4 %multiply_convert_fusion.3 = (bf16[512,2048]{1,0:T(8,128)(2,1)S(1)}, bf16[512,2048]{1,0:T(8,128)(2,1)S(1)}) fusion(f32[2048]{0:T(1024)S(1)} %get-tuple-element.172, f32[8,2048]{1,0:T(8,128)S(1)} %get-tuple-element.174, f32[8,4096]{1,0:T(8,128)} %get-tuple-element.173, s32[]{:T(128)S(6)} %select_n.9), kind=kOutput, calls=%fused_computation.2.clone.1 | convolution fusion | flops 104857600 | bytes 4284420 | tf_op jit(solution)/shard_map/while/body/eval_jaxpr/dot_general | solution.py:21
  127.4 20.4 %multiply_convert_fusion.3 = (bf16[512,2048]{1,0:T(8,128)(2,1)S(1)}, bf16[512,2048]{1,0:T(8,128)(2,1)S(1)}) fusion(f32[2048]{0:T(1024)S(1)} %get-tuple-element.172, f32[8,2048]{1,0:T(8,128)S(1)} %get-tuple-element.174, f32[8,4096]{1,0:T(8,128)} %get-tuple-element.173, s32[]{:T(128)S(6)} %select_n.9), kind=kOutput, calls=%fused_computation.2.clone.1 | convolution fusion | flops 104857600 | bytes 4284420 | tf_op jit(solution)/shard_map/while/body/eval_jaxpr/dot_general | solution.py:21
  150.2 20.4 %multiply_convert_fusion.3 = (bf16[512,2048]{1,0:T(8,128)(2,1)S(1)}, bf16[512,2048]{1,0:T(8,128)(2,1)S(1)}) fusion(f32[2048]{0:T(1024)S(1)} %get-tuple-element.172, f32[8,2048]{1,0:T(8,128)S(1)} %get-tuple-element.174, f32[8,4096]{1,0:T(8,128)} %get-tuple-element.173, s32[]{:T(128)S(6)} %select_n.9), kind=kOutput, calls=%fused_computation.2.clone.1 | convolution fusion | flops 104857600 | bytes 4284420 | tf_op jit(solution)/shard_map/while/body/eval_jaxpr/dot_general | solution.py:21
  170.6 2.5 maximum_dynamic-update-slice_fusion.2
  173.1 20.4 %multiply_convert_fusion.3 = (bf16[512,2048]{1,0:T(8,128)(2,1)S(1)}, bf16[512,2048]{1,0:T(8,128)(2,1)S(1)}) fusion(f32[2048]{0:T(1024)S(1)} %get-tuple-element.172, f32[8,2048]{1,0:T(8,128)S(1)} %get-tuple-element.174, f32[8,4096]{1,0:T(8,128)} %get-tuple-element.173, s32[]{:T(128)S(6)} %select_n.9), kind=kOutput, calls=%fused_computation.2.clone.1 | convolution fusion | flops 104857600 | bytes 4284420 | tf_op jit(solution)/shard_map/while/body/eval_jaxpr/dot_general | solution.py:21
  196.2 13.5 %fusion.5 = f32[32,4096]{1,0:T(8,128)S(1)} fusion(bf16[4096,4096]{1,0:T(8,128)(2,1)} %get-tuple-element.96, f32[31,4096]{1,0:T(8,128)S(1)} %add_convert_fusion, f32[1,4096]{1,0:T(1,128)S(1)} %bitcast.11), kind=kOutput, calls=%fused_computation.19 | convolution fusion | flops 1074266112 | bytes 34603008 | tf_op jit(solution)/shard_map/dot_general | solution.py:53
  209.7 146.9 %all-reduce.4 = (bf16[32,4096]{1,0:T(8,128)(2,1)S(1)}, f32[32]{0:T(128)S(1)}) all-reduce(f32[32,4096]{1,0:T(8,128)S(1)} %fusion.5, f32[32]{0:T(128)S(1)} %multiply_reduce_fusion.4), channel_id=1, replica_groups=mesh['rows'=32,'feat'=8] {'rows'}, use_global_device_ids=true, to_apply=%region_4.0 | all-reduce | flops 131104 | bytes 786688 | tf_op jit(solution)/shard_map/psum | solution.py:54
  356.6 15.3 %fusion.8 = f32[32,4096]{1,0:T(8,128)S(1)} fusion(bf16[32,4096]{1,0:T(8,128)(2,1)S(1)} %get-tuple-element.109, bf16[4096,4096]{1,0:T(8,128)(2,1)} %get-tuple-element.96), kind=kOutput, calls=%fused_computation.26 | convolution fusion | flops 1073741824 | bytes 34340864 | tf_op jit(solution)/shard_map/dot_general | solution.py:56
  375.7 12.4 %collective-permute-done.1 = f32[32,4096]{1,0:T(8,128)S(1)} collective-permute-done((f32[32,4096]{1,0:T(8,128)S(1)}, f32[32,4096]{1,0:T(8,128)S(1)}, u32[]{:S(2)}, u32[]{:S(2)}) %collective-permute-start.1) | collective-permute-done | bytes 524320 | tf_op jit(solution)/shard_map/ppermute | solution.py:64
  388.2 3.3 collective-permute-start.2
  391.6 18.1 %psum.54 = f32[32]{0:T(128)S(1)} all-reduce(f32[32]{0:T(128)S(1)} %multiply_reduce_fusion.3), channel_id=1, replica_groups=mesh['rows'=32,'feat'=8] {'feat'}, use_global_device_ids=true, to_apply=%region_6.0 | all-reduce | flops 32 | bytes 256 | tf_op jit(solution)/shard_map/psum | solution.py:65
  410.0 75.4 %psum.55 = f32[32]{0:T(128)S(1)} all-reduce(f32[32]{0:T(128)S(1)} %get-tuple-element.111), channel_id=1, replica_groups=mesh['rows'=32,'feat'=8] {'rows'}, use_global_device_ids=true, to_apply=%region_8.0 | all-reduce | flops 32 | bytes 256 | tf_op jit(solution)/shard_map/psum | solution.py:37
  485.4 13.6 %fusion.3 = f32[32,4096]{1,0:T(8,128)S(1)} fusion(bf16[4096,4096]{1,0:T(8,128)(2,1)} %get-tuple-element.96, f32[32,4096]{1,0:T(8,128)S(1)} %get-tuple-element.112, f32[32]{0:T(128)S(1)} %div.18, f32[31,4096]{1,0:T(8,128)S(1)} %add_convert_fusion, f32[1,4096]{1,0:T(1,128)S(1)} %bitcast.13), kind=kOutput, calls=%fused_computation.17 | convolution fusion | flops 1074266112 | bytes 35127424 | tf_op jit(solution)/shard_map/dot_general | solution.py:53
  499.3 140.5 %all-reduce.5 = (bf16[32,4096]{1,0:T(8,128)(2,1)S(1)}, f32[32]{0:T(128)S(1)}) all-reduce(f32[32,4096]{1,0:T(8,128)S(1)} %fusion.3, f32[32]{0:T(128)S(1)} %multiply_reduce_fusion), channel_id=1, replica_groups=mesh['rows'=32,'feat'=8] {'rows'}, use_global_device_ids=true, to_apply=%region_9.0 | all-reduce | flops 131104 | bytes 786688 | tf_op jit(solution)/shard_map/psum | solution.py:54
  639.7 15.3 %fusion.9 = f32[32,4096]{1,0:T(8,128)S(1)} fusion(bf16[32,4096]{1,0:T(8,128)(2,1)S(1)} %get-tuple-element.107, bf16[4096,4096]{1,0:T(8,128)(2,1)} %get-tuple-element.96), kind=kOutput, calls=%fused_computation.27 | convolution fusion | flops 1073741824 | bytes 34340864 | tf_op jit(solution)/shard_map/dot_general | solution.py:56
  658.5 12.7 %collective-permute-done.4 = f32[32,4096]{1,0:T(8,128)S(1)} collective-permute-done((f32[32,4096]{1,0:T(8,128)S(1)}, f32[32,4096]{1,0:T(8,128)S(1)}, u32[]{:S(2)}, u32[]{:S(2)}) %collective-permute-start.4) | collective-permute-done | bytes 524320 | tf_op jit(solution)/shard_map/ppermute | solution.py:64
  672.9 18.5 %psum.57 = f32[32]{0:T(128)S(1)} all-reduce(f32[32]{0:T(128)S(1)} %multiply_reduce_fusion.1), channel_id=1, replica_groups=mesh['rows'=32,'feat'=8] {'feat'}, use_global_device_ids=true, to_apply=%region_11.0 | all-reduce | flops 32 | bytes 256 | tf_op jit(solution)/shard_map/psum | solution.py:65
  (35 shorter events, 27.5 us)
Async XLA Ops:
  13.1 182.7 %copy-start.1 = (s32[31,4096]{1,0:T(8,128)S(1)}, s32[31,4096]{1,0:T(8,128)}, u32[]{:S(2)}) copy-start(s32[31,4096]{1,0:T(8,128)} %param.11) | copy-start | bytes 1523716
  13.1 182.8 %copy-start = (f32[4096]{0:T(1024)S(1)}, f32[4096]{0:T(1024)}, u32[]{:S(2)}) copy-start(f32[4096]{0:T(1024)} %param.10) | copy-start | bytes 49156
  371.9 2.0 collective-permute-start
  374.0 14.1 %collective-permute-start.1 = (f32[32,4096]{1,0:T(8,128)S(1)}, f32[32,4096]{1,0:T(8,128)S(1)}, u32[]{:S(2)}, u32[]{:S(2)}) collective-permute-start(f32[32,4096]{1,0:T(8,128)S(1)} %add.77), channel_id=1, source_target_pairs={{0,2},{1,3},{2,0},{3,1},{4,6},{5,7},{6,4},{7,5},{8,10},{9,11},{10,... | collective-permute-start | bytes 1572872 | tf_op jit(solution)/shard_map/ppermute | solution.py:64
  388.2 21.5 %collective-permute-start.2 = (f32[32,4096]{1,0:T(8,128)S(1)}, f32[32,4096]{1,0:T(8,128)S(1)}, u32[]{:S(2)}, u32[]{:S(2)}) collective-permute-start(f32[32,4096]{1,0:T(8,128)S(1)} %add.78), channel_id=1, source_target_pairs={{0,4},{1,5},{2,6},{3,7},{4,0},{5,1},{6,2},{7,3},{8,12},{9,13},{10,... | collective-permute-start | bytes 1572872 | tf_op jit(solution)/shard_map/ppermute | solution.py:64
  655.1 2.0 collective-permute-start.3
  657.1 14.1 %collective-permute-start.4 = (f32[32,4096]{1,0:T(8,128)S(1)}, f32[32,4096]{1,0:T(8,128)S(1)}, u32[]{:S(2)}, u32[]{:S(2)}) collective-permute-start(f32[32,4096]{1,0:T(8,128)S(1)} %add.84), channel_id=1, source_target_pairs={{0,2},{1,3},{2,0},{3,1},{4,6},{5,7},{6,4},{7,5},{8,10},{9,11},{10,... | collective-permute-start | bytes 1572872 | tf_op jit(solution)/shard_map/ppermute | solution.py:64
  671.3 20.2 %collective-permute-start.5 = (f32[32,4096]{1,0:T(8,128)S(1)}, f32[32,4096]{1,0:T(8,128)S(1)}, u32[]{:S(2)}, u32[]{:S(2)}) collective-permute-start(f32[32,4096]{1,0:T(8,128)S(1)} %add.85), channel_id=1, source_target_pairs={{0,4},{1,5},{2,6},{3,7},{4,0},{5,1},{6,2},{7,3},{8,12},{9,13},{10,... | collective-permute-start | bytes 1572872 | tf_op jit(solution)/shard_map/ppermute | solution.py:64
